TPU v7x, 32 devices: a whole 2x2x4 slice. The times are simulated.
32 devices in a mesh: parts: 2 (over y), tp: 4 (over z), sec: 4 (over x, core).
Axes of the slice: x: 2, y: 2, z: 4, core: 2. Of those that a mesh axis runs over, the one named last changes fastest.
Arguments:
- queries: bfloat16 [256, 8192], P(('parts', 'sec', 'tp')), parts along dimension 0, may hold values from -64 to 64
- keys: bfloat16 [256, 256, 1024], P(('parts', 'sec', 'tp')), parts along dimension 0, may hold values from -6 to 6
- values: bfloat16 [256, 256, 1024], P(('parts', 'sec', 'tp')), parts along dimension 0, may hold values from -6 to 6
- lengths: int32 [256], P(('parts', 'sec', 'tp')), parts along dimension 0, may hold values from 2 to 256, as said below
- batch_of_slot: int32 [256], P('parts'), parts along dimension 0, may hold values from 0 to 127, each once
- residual: bfloat16 [256, 8192], P('parts', 'sec'), parts along dimension 0, may hold values from -16 to 16
- out_weight: bfloat16 [8192, 8192], P('tp', 'sec'), may hold values from -0.25 to 0.25
- norm_gain: float32 [8192], P('sec'), may hold values from 0.1 to 1.9
- gate_weight: bfloat16 [8192, 14336], P('sec', 'tp'), may hold values from -0.0625 to 0.0625
- up_weight: bfloat16 [8192, 14336], P('sec', 'tp'), may hold values from -0.0625 to 0.0625
- down_weight: bfloat16 [14336, 8192], P('tp', 'sec'), may hold values from -0.046875 to 0.046875
Outputs:
- layer_out: bfloat16 [256, 8192], P(('parts', 'sec', 'tp')), parts along dimension 0
There are 2 independent parts, one for each index of `parts`. A program takes and returns all parts, laid end to end along the dimension named above; an argument that names none is the same for every part. Nothing has to cross between parts.
Inputs may be any that keep to these rules, and one draw needn't show every extreme that they name: `lengths`: some request has exactly 256 valid positions. `batch_of_slot`: each batch row appears once.
All inputs are finite; a program needn't handle non-finite values.
Results may differ from a plain program's by a relative error of at most 0.0051.
Values may be sent and summed in bfloat16 or wider, within the bound.
A program may use at most 192 MiB of HBM per device.

v0:
```python
import jax
import jax.numpy as jnp
from jax import lax
from jax.sharding import PartitionSpec as P

D = 8192
QUERY_HEADS = 64
KEY_VALUE_HEADS = 8
HEAD_WIDTH = 128


epsilon = 1e-05


def attend(queries, keys, values, lengths):
    request_list = queries.shape[0]
    every_position = keys.shape[1]
    group_width = QUERY_HEADS // KEY_VALUE_HEADS
    query_table = queries.reshape(request_list, KEY_VALUE_HEADS, group_width, HEAD_WIDTH)
    key_table = keys.reshape(request_list, every_position, KEY_VALUE_HEADS, HEAD_WIDTH)
    value_table = values.reshape(request_list, every_position, KEY_VALUE_HEADS, HEAD_WIDTH)
    scores = jnp.einsum(
        "rkgd,rpkd->rkgp", query_table, key_table, preferred_element_type=jnp.float32
    ) * HEAD_WIDTH ** (-0.5)
    positions = lax.broadcasted_iota(jnp.int32, scores.shape, 3)
    in_cache = positions < lengths[:, None, None, None]
    scores = jnp.where(in_cache, scores, -jnp.inf)
    row_max = jnp.max(scores, axis=3, keepdims=True)
    weights = jnp.exp(scores - row_max)
    probabilities = (weights / jnp.sum(weights, axis=3, keepdims=True)).astype(jnp.bfloat16)
    attended = jnp.einsum(
        "rkgp,rpkd->rkgd", probabilities, value_table, preferred_element_type=jnp.float32
    )
    return attended.astype(jnp.bfloat16).reshape(request_list, QUERY_HEADS * HEAD_WIDTH)


def normalize(hidden_state, norm_gain):
    squares = jnp.sum(hidden_state * hidden_state, axis=-1)
    totals = lax.psum(squares, "sec")
    scale_rows = lax.rsqrt(totals / D + epsilon)
    return (hidden_state * scale_rows[..., None] * norm_gain).astype(jnp.bfloat16)


def local(
    queries,
    keys,
    values,
    lengths,
    batch_of_slot,
    residual,
    out_weight,
    norm_gain,
    gate_weight,
    up_weight,
    down_weight,
):
    request_list = queries.shape[0]
    tp_count = lax.axis_size("tp")
    sec_count = lax.axis_size("sec")
    width_part = residual.shape[1]
    tp_rank = lax.axis_index("tp")
    attended = attend(queries, keys, values, lengths)
    columns_in = lax.all_to_all(attended, "tp", split_axis=1, concat_axis=0, tiled=True)
    columns_in = columns_in.reshape(tp_count, request_list, columns_in.shape[1])
    partial_out = jnp.einsum(
        "tnc,cd->tnd",
        lax.all_gather(columns_in, "sec", axis=1, tiled=True),
        out_weight,
        preferred_element_type=jnp.float32,
    )
    slot_rows = jnp.take(residual, batch_of_slot, axis=0)
    arranged = slot_rows.reshape(sec_count, tp_count, request_list, width_part).transpose(
        1, 0, 2, 3
    )
    arranged = arranged.reshape(tp_count, sec_count * request_list, width_part).astype(jnp.float32)
    full_state = arranged + lax.psum(partial_out, "tp")
    normed = normalize(full_state, norm_gain)
    own_state = lax.dynamic_slice_in_dim(full_state, tp_rank, 1, 0)
    flat_normed = normed.reshape(-1, width_part)
    gate_part = jnp.dot(flat_normed, gate_weight, preferred_element_type=jnp.float32)
    up_part = jnp.dot(flat_normed, up_weight, preferred_element_type=jnp.float32)
    gate_full, up_full = lax.psum((gate_part, up_part), "sec")
    hidden_units = (jax.nn.silu(gate_full) * up_full).astype(jnp.bfloat16)
    ffn_out = lax.psum_scatter(
        jnp.dot(hidden_units, down_weight, preferred_element_type=jnp.float32),
        "tp",
        scatter_dimension=0,
        tiled=True,
    )
    layer_rows = (own_state[0] + ffn_out).astype(jnp.bfloat16)
    return lax.all_to_all(layer_rows, "sec", split_axis=0, concat_axis=1, tiled=True)


def solution(mesh):
    return jax.shard_map(
        local,
        mesh=mesh,
        in_specs=(
            P(("parts", "sec", "tp"), None),
            P(("parts", "sec", "tp"), None, None),
            P(("parts", "sec", "tp"), None, None),
            P(("parts", "sec", "tp")),
            P("parts"),
            P("parts", "sec"),
            P("tp", "sec"),
            P("sec"),
            P("sec", "tp"),
            P("sec", "tp"),
            P("tp", "sec"),
        ),
        out_specs=P(("parts", "sec", "tp"), None),
        check_vma=False,
    )
```

profile of v0, /device:TPU:29, one launch (start us, length us, event | category | flops | bytes accessed | tf_op | source)
XLA Modules:
  0.0 236.2 jit_solution(2143987416513814454)
XLA Ops:
  6.5 0.0 copy-start
  6.5 0.0 all-reduce.4.cloned.1.call-start
  6.5 3.6 %fusion.27 = (f32[8,8,8]{2,1,0:T(8,128)S(1)}, f32[8,8,8,256]{3,2,1,0:T(8,128)S(1)}) fusion(s32[8]{0:T(128)} %param.14, bf16[8,8,8,128]{3,0,2,1:T(8,128)(2,1)} %bitcast.61, bf16[8,256,1024]{2,1,0:T(8,128)(2,1)} %param.12), kind=kOutput, calls=%fused_computation.34 | convolution fusion | flops 34210048 | bytes 4851744 | tf_op jit(solution)/shard_map/sub | solution.py:29
  10.1 2.9 %fusion.17 = bf16[8,8,8,128]{3,2,1,0:T(8,128)(2,1)S(1)} fusion(f32[8,8,8,256]{3,2,1,0:T(8,128)S(1)} %get-tuple-element.10, f32[8,8,8]{2,1,0:T(8,128)S(1)} %get-tuple-element.9, bf16[8,256,1024]{2,1,0:T(8,128)(2,1)} %param.13), kind=kOutput, calls=%fused_computation.15 | convolution fusion | flops 33882112 | bytes 4851712 | tf_op jit(solution)/shard_map/rkgp,rpkd->rkgd/dot_general | solution.py:31
  13.1 0.1 copy.17
  13.2 8.0 %all_to_all.35 = bf16[8,4,2048]{2,0,1:T(8,128)(2,1)S(1)} all-to-all(bf16[8,4,2048]{2,0,1:T(8,128)(2,1)S(1)} %copy.17), channel_id=1, replica_groups=mesh['parts'=2,'tp'=4,'sec'=4] {'tp'}, dimensions={1} | all-to-all | bytes 262144 | tf_op jit(solution)/shard_map/all_to_all | solution.py:63
  21.2 8.2 %all_gather.3 = bf16[4,32,2048]{2,1,0:T(8,128)(2,1)S(1)} all-gather(bf16[4,8,2048]{2,1,0:T(8,128)(2,1)S(1)} %bitcast.59), channel_id=1, replica_groups=mesh['parts'=2,'tp'=4,'sec'=4] {'sec'}, dimensions={1}, use_global_device_ids=true | all-gather | bytes 655360 | tf_op jit(solution)/shard_map/all_gather | solution.py:67
  29.4 0.0 copy-start.3
  29.4 5.7 %fusion.1 = f32[4,32,2048]{2,1,0:T(8,128)} fusion(bf16[4,32,2048]{2,1,0:T(8,128)(2,1)S(1)} %all_gather.3, bf16[2048,2048]{1,0:T(8,128)(2,1)} %param.17), kind=kOutput, calls=%fused_computation.2 | convolution fusion | flops 1073741824 | bytes 9961472 | tf_op jit(solution)/shard_map/tnc,cd->tnd/dot_general | solution.py:65
  35.1 0.0 copy-start.2
  35.1 0.0 all-reduce.4.cloned.1.call-update
  35.2 0.0 all-reduce.6.cloned.1.call-start
  35.2 0.0 copy-done.3
  35.2 0.1 broadcast_in_dim.23
  35.4 0.0 copy-done
  35.4 0.9 gather_fusion
  36.3 49.2 %all-reduce.4.cloned.1.call-done = f32[4,32,2048]{2,1,0:T(8,128)} async-done(((f32[4,32,2048]{2,1,0:T(8,128)}), f32[4,32,2048]{2,1,0:T(8,128)}) %all-reduce.4.cloned.1.call-update) | async-done | bytes 1048592 | tf_op jit(solution)/shard_map/psum | solution.py:76
  85.5 0.0 slice-start
  85.5 2.6 %multiply_reduce_fusion = (f32[4,32]{1,0:T(4,128)S(1)}, f32[4,32,2048]{2,1,0:T(8,128)}) fusion(f32[4,32,2048]{2,1,0:T(8,128)} %all-reduce.4.cloned.1.call-done, bf16[4,4,8,2048]{3,2,1,0:T(8,128)(2,1)S(1)} %bitcast.58, pred[4,4,8]{2,0,1:T(4,128)(4,1)S(1)} %copy.12), kind=kLoop, calls=%fused_computation.18 | loop fusion | flops 1310592 | bytes 2622080 | tf_op jit(solution)/shard_map/reduce_sum | solution.py:38
  88.2 5.5 %psum.29 = f32[4,32]{1,0:T(4,128)S(1)} all-reduce(f32[4,32]{1,0:T(4,128)S(1)} %get-tuple-element.7), channel_id=1, replica_groups=mesh['parts'=2,'tp'=4,'sec'=4] {'sec'}, use_global_device_ids=true, to_apply=%region_4.5 | all-reduce | flops 128 | bytes 1024 | tf_op jit(solution)/shard_map/psum | solution.py:39
  93.7 0.0 copy-done.2
  93.7 1.4 multiply_convert_fusion.1
  95.0 0.0 slice-start.1
  95.1 0.0 slice-start.2
  95.1 0.0 slice-start.3
  95.1 8.7 %fusion.32 = f32[128,3584]{1,0:T(8,128)} fusion(bf16[128,2048]{1,0:T(8,128)(2,1)S(1)} %bitcast.56, bf16[2048,3584]{1,0:T(8,128)(2,1)} %param.19), kind=kOutput, calls=%fused_computation.35 | convolution fusion | flops 1879048192 | bytes 17039360 | tf_op jit(solution)/shard_map/dot_general | solution.py:80
  103.8 0.0 slice-done
  103.8 0.0 slice-done.1
  103.8 0.0 slice-done.2
  103.8 0.8 slice-done.3
  104.6 3.3 %fusion.33 = f32[128,3584]{1,0:T(8,128)} fusion(bf16[128,2048]{1,0:T(8,128)(2,1)S(1)} %bitcast.57, bf16[2048,3584]{1,0:T(8,128)(2,1)S(1)} %bitcast.55), kind=kOutput, calls=%fused_computation.36 | convolution fusion | flops 1879048192 | bytes 17039360 | tf_op jit(solution)/shard_map/dot_general | solution.py:81
  107.9 0.0 all-reduce.6.cloned.1.call-update
  107.9 0.0 reduce-scatter.2.cloned.1.call-start
  107.9 78.3 %all-reduce.6.cloned.1.call-done = (f32[128,3584]{1,0:T(8,128)}, f32[128,3584]{1,0:T(8,128)}) async-done(((f32[128,3584]{1,0:T(8,128)}, f32[128,3584]{1,0:T(8,128)}), (f32[128,3584]{1,0:T(8,128)}, f32[128,3584]{1,0:T(8,128)})) %all-reduce.6.cloned.1.call-update) | async-done | bytes 3670032 | tf_op jit(solution)/shard_map/psum | solution.py:82
  186.3 0.0 copy-start.1
  186.3 9.5 %fusion.20 = f32[128,2048]{1,0:T(8,128)} fusion(bf16[3584,2048]{1,0:T(8,128)(2,1)} %param.21, f32[128,3584]{1,0:T(8,128)} %get-tuple-element.5, f32[128,3584]{1,0:T(8,128)} %get-tuple-element.6), kind=kOutput, calls=%fused_computation.19 | convolution fusion | flops 1881800704 | bytes 19398656 | tf_op jit(solution)/shard_map/dot_general | solution.py:85
  195.8 0.0 reduce-scatter.2.cloned.1.call-update
  195.8 24.9 %reduce-scatter.2.cloned.1.call-done = f32[32,2048]{1,0:T(8,128)} async-done(((f32[128,2048]{1,0:T(8,128)}), f32[32,2048]{1,0:T(8,128)}) %reduce-scatter.2.cloned.1.call-update) | async-done | bytes 262160 | tf_op jit(solution)/shard_map/reduce_scatter | solution.py:84
  220.7 1.1 fusion.24
  221.8 7.2 %all_to_all.36 = bf16[4,8,2048]{2,1,0:T(8,128)(2,1)S(1)} all-to-all(bf16[4,8,2048]{2,1,0:T(8,128)(2,1)S(1)} %fusion.24), channel_id=1, replica_groups=mesh['parts'=2,'tp'=4,'sec'=4] {'sec'}, dimensions={0} | all-to-all | bytes 262144 | tf_op jit(solution)/shard_map/all_to_all | solution.py:91
  229.0 0.7 copy.48
  229.6 0.0 copy-done.1
  (7 shorter events, 0.1 us)
Async XLA Ops:
  6.5 28.8 %copy-start = (bf16[128,2048]{1,0:T(8,128)(2,1)S(1)}, bf16[128,2048]{1,0:T(8,128)(2,1)}, u32[]{:S(2)}) copy-start(bf16[128,2048]{1,0:T(8,128)(2,1)} %param.16) | copy-start | bytes 1572868
  6.5 79.0 %all-reduce.4.cloned.1.call-start = ((), (), s32[]{:S(2)}) async-start(), calls=%async_computation.3 | async-start | bytes 2097152 | tf_op jit(solution)/shard_map/psum | solution.py:76
  29.4 5.8 %copy-start.3 = (s32[128]{0:T(128)S(1)}, s32[128]{0:T(128)}, u32[]{:S(2)}) copy-start(s32[128]{0:T(128)} %param.15) | copy-start | bytes 1540
  35.1 58.5 %copy-start.2 = (f32[2048]{0:T(1024)S(1)}, f32[2048]{0:T(1024)}, u32[]{:S(2)}) copy-start(f32[2048]{0:T(1024)} %param.18) | copy-start | bytes 24580
  35.2 151.1 %all-reduce.6.cloned.1.call-start = ((), (), s32[]{:S(2)}) async-start(), calls=%async_computation.5 | async-start | bytes 7340032 | tf_op jit(solution)/shard_map/psum | solution.py:82
  85.5 18.2 %slice-start = ((s8[14680064]{0:T(1024)(128)(4,1)}), s8[2097152]{0:T(1024)(128)(4,1)S(1)}, s32[]{:S(2)}) async-start(s8[14680064]{0:T(1024)(128)(4,1)} %bitcast.54), calls=%async_computation.6 | async-start | bytes 4194304
  95.0 8.7 %slice-start.1 = ((s8[14680064]{0:T(1024)(128)(4,1)}), s8[4194304]{0:T(1024)(128)(4,1)S(1)}, s32[]{:S(2)}) async-start(s8[14680064]{0:T(1024)(128)(4,1)} %bitcast.54), calls=%async_computation.7 | async-start | bytes 8388608
  95.1 8.7 %slice-start.2 = ((s8[14680064]{0:T(1024)(128)(4,1)}), s8[4194304]{0:T(1024)(128)(4,1)S(1)}, s32[]{:S(2)}) async-start(s8[14680064]{0:T(1024)(128)(4,1)} %bitcast.54), calls=%async_computation.8 | async-start | bytes 8388608
  95.1 9.5 %slice-start.3 = ((s8[14680064]{0:T(1024)(128)(4,1)}), s8[4194304]{0:T(1024)(128)(4,1)S(1)}, s32[]{:S(2)}) async-start(s8[14680064]{0:T(1024)(128)(4,1)} %bitcast.54), calls=%async_computation.9 | async-start | bytes 8388608
  107.9 112.8 %reduce-scatter.2.cloned.1.call-start = ((), (), s32[]{:S(2)}) async-start(), calls=%async_computation.4 | async-start | bytes 1310720 | tf_op jit(solution)/shard_map/reduce_scatter | solution.py:84
  186.3 43.3 %copy-start.1 = (bf16[128,2048]{1,0:T(8,128)(2,1)S(1)}, bf16[128,2048]{1,0:T(8,128)(2,1)}, u32[]{:S(2)}) copy-start(bf16[128,2048]{1,0:T(8,128)(2,1)} %param.16) | copy-start | bytes 1572868
Sparse Core Ops, SparseCore 0:
  35.3 50.2 all-reduce.3
  108.0 78.2 all-reduce.5
  195.9 24.7 reduce-scatter.1
where the time goes:
time: 241 us; the launch traced here: 236 us
  waiting for transfers between devices  153 us (63%)
  matrix products  33.7 us (14%)
  blocking collectives  28.9 us (12%)
  between operations  13.2 us (5%)
  other arithmetic  5.07 us (2%)
  local copies, waits for them, and re-layouts  2.63 us (1%)
    psum x1, waiting for transfers between devices, local(): gate_full, up_full = lax.psum((gate_part, up_part), 'sec')  78.3 us
    psum x1, waiting for transfers between devices, local(): full_state = arranged + lax.psum(partial_out, 'tp')  49.2 us
    reduce_scatter x1, waiting for transfers between devices, local(): lax.psum_scatter(jnp.dot(hidden_units, down_weight, preferred_element_typ...  24.9 us
    dot_general x1, matrix products, local(): jnp.dot(hidden_units, down_weight, preferred_element_type=jnp.float32)  9.5 us
    dot_general x1, matrix products, local(): jnp.dot(flat_normed, gate_weight, preferred_element_type=jnp.float32)  8.68 us
    all_gather x1, blocking collectives, local(): lax.all_gather(columns_in, 'sec', axis=1, tiled=True)  8.24 us
    all_to_all x1, blocking collectives, local(): lax.all_to_all(attended, 'tp', split_axis=1, concat_axis=0, tiled=True)  8.02 us
    all_to_all x1, blocking collectives, local(): lax.all_to_all(layer_rows, 'sec', split_axis=0, concat_axis=1, tiled=True)  7.17 us
  transfers between devices with their start and end apart: 3, of which 3 were waited for; matrix products, arithmetic and copies ran while one was open for 0% of the time, Pallas kernels for 0%

commit v1 on v0

v1 whole, which is shorter than its diff:
```python
import functools

import jax
import jax.numpy as jnp
from jax import lax
from jax.experimental import pallas as pl
from jax.experimental.pallas import tpu as pltpu
from jax.sharding import PartitionSpec as P

QUERY_HEADS = 64
KEY_VALUE_HEADS = 8
HEAD_WIDTH = 128
EPSILON = 1e-05
MESH = pl.DeviceIdType.MESH
BF16 = jnp.bfloat16
F32 = jnp.float32
LAG_SUM, LAG_HIDDEN, LAG_FORWARD, LAG_DOWN = 1, 3, 5, 6
OWN_RING = 4


def attend(queries, keys, values, lengths):
    request_list = queries.shape[0]
    every_position = keys.shape[1]
    group_width = QUERY_HEADS // KEY_VALUE_HEADS
    query_table = queries.reshape(request_list, KEY_VALUE_HEADS, group_width, HEAD_WIDTH)
    key_table = keys.reshape(request_list, every_position, KEY_VALUE_HEADS, HEAD_WIDTH)
    value_table = values.reshape(request_list, every_position, KEY_VALUE_HEADS, HEAD_WIDTH)
    scores = jnp.einsum(
        "rkgd,rpkd->rkgp", query_table, key_table, preferred_element_type=jnp.float32
    ) * HEAD_WIDTH ** (-0.5)
    positions = lax.broadcasted_iota(jnp.int32, scores.shape, 3)
    in_cache = positions < lengths[:, None, None, None]
    scores = jnp.where(in_cache, scores, -jnp.inf)
    row_max = jnp.max(scores, axis=3, keepdims=True)
    weights = jnp.exp(scores - row_max)
    probabilities = (weights / jnp.sum(weights, axis=3, keepdims=True)).astype(jnp.bfloat16)
    attended = jnp.einsum(
        "rkgp,rpkd->rkgd", probabilities, value_table, preferred_element_type=jnp.float32
    )
    return attended.astype(jnp.bfloat16).reshape(request_list, QUERY_HEADS * HEAD_WIDTH)


def pieces(size):
    return size // 512 if size % 512 == 0 else size // 128


def layer_kernel(
    n, s, r,
    att_ref, res_ref, gain_ref, ow_hbm, gw_hbm, uw_hbm, dw_hbm,
    out_ref,
    ow, gw, uw, dw, cols, xin, part32, part16, rs, state, sqs, nf,
    gu32, gsend, grecv, gown, xsend, xrecv, hid, acc, dsend, drecv, fin, outs,
    ow_sem, gw_sem, uw_sem, dw_sem, own_sem,
    a1_send, a2_send, a_recv, rs_send, rs_recv, sq_send, sq_recv, nf_send, nf_recv,
    g_send, g_recv, x_send, x_recv, h_send, h_recv, d_send, d_recv, f_send, f_recv,
):
    X = s // 2
    R = s * r
    C = ow.shape[0]
    W = ow.shape[1]
    K, M, fc = hid.shape
    Q = n * r
    NC = part32.shape[0]
    wc = W // NC
    D = C * n
    t = lax.axis_index("tp")
    j = lax.axis_index("sec")
    x = j // 2
    c = j % 2
    mate = x * 2 + (1 - c)

    def tp_at(d):
        return lax.rem(t + d, n)

    def sec_at(d):
        return lax.rem(j + d, s)

    def x_at(d):
        return lax.rem(x + d, X)

    def remote(src, dst, send, recv, **where):
        return pltpu.make_async_remote_copy(
            src_ref=src, dst_ref=dst, send_sem=send, recv_sem=recv,
            device_id=where, device_id_type=MESH,
        )

    def rows(index, count):
        return pl.ds(pl.multiple_of(index * count, count), count)

    def ow_copy(i):
        at = pl.ds(i * (C // 4), C // 4)
        return pltpu.make_async_copy(ow_hbm.at[at], ow.at[at], ow_sem.at[i])

    def gw_copy(k):
        at = pl.ds(pl.multiple_of(k * fc, fc), fc)
        return pltpu.make_async_copy(gw_hbm.at[:, at], gw.at[k], gw_sem.at[k])

    def uw_copy(k):
        at = pl.ds(pl.multiple_of(k * fc, fc), fc)
        return pltpu.make_async_copy(uw_hbm.at[:, at], uw.at[k], uw_sem.at[k])

    def dw_copy(k):
        return pltpu.make_async_copy(dw_hbm.at[rows(k, fc)], dw.at[k], dw_sem.at[k])

    for i in range(4):
        ow_copy(i).start()

    barrier = pltpu.get_barrier_semaphore()
    for d in range(1, n):
        pl.semaphore_signal(barrier, inc=1, device_id={"tp": tp_at(d)}, device_id_type=MESH)
    for d in range(1, s):
        pl.semaphore_signal(barrier, inc=1, device_id={"sec": sec_at(d)}, device_id_type=MESH)
    pl.semaphore_wait(barrier, n + s - 2)

    def feature(tt):
        return att_ref.at[:, pl.ds(pl.multiple_of(tt * C, C), C)]

    def a1(d):
        return remote(feature(tp_at(d)), cols.at[t, j], a1_send.at[d - 1], a_recv.at[t, j], tp=tp_at(d))

    def a1_arrive(tt):
        return remote(cols.at[tt, j], cols.at[tt, j], a1_send.at[0], a_recv.at[tt, j], tp=tp_at(1))

    def a2_block(tt, jj, own=False):
        return feature(t) if own else cols.at[tt, jj]

    def a2_mate(tt, jj, own=False):
        return remote(a2_block(tt, jj, own), cols.at[tt, jj], a2_send.at[tt, jj], a_recv.at[tt, jj], sec=mate)

    def a2_x(tt, d, own=False):
        return remote(
            a2_block(tt, j, own), cols.at[tt, j], a2_send.at[tt, s - 1 + d],
            a_recv.at[tt, j], sec=x_at(d) * 2 + c,
        )

    for d in range(1, n):
        a1(d).start()
    own_copy = pltpu.make_async_copy(feature(t), cols.at[t, j], own_sem)
    own_copy.start()
    for d in range(1, X):
        a2_x(t, d, True).start()
    a2_mate(t, j, True).start()
    for k in range(K):
        gw_copy(k).start()
        uw_copy(k).start()
    for k in range(K):
        dw_copy(k).start()
    for d in range(1, n):
        tt = tp_at(d)
        a1_arrive(tt).wait_recv()
        for e in range(1, X):
            a2_x(tt, e).start()
        a2_mate(tt, j).start()
    for d in range(n):
        tt = tp_at(d)
        for e in range(1, X):
            jj = x_at(e) * 2 + c
            a2_mate(tt, jj).wait_recv()
            a2_mate(tt, jj).start()
    own_copy.wait()
    for d in range(n):
        tt = tp_at(d)
        for e in range(X):
            a2_mate(tt, x_at(e) * 2 + (1 - c)).wait_recv()
    for tt in range(n):
        xin[tt * R:(tt + 1) * R, :] = cols[tt].astype(F32).reshape(R, C).astype(BF16)

    def rs_copy(i, d):
        return remote(
            part16.at[i, rows(tp_at(d), R)], rs.at[i, d - 1],
            rs_send.at[i, d - 1], rs_recv.at[i, d - 1], tp=tp_at(d),
        )

    for i in range(4):
        ow_copy(i).wait()

    @pl.loop(0, NC)
    def _(i):
        at = pl.ds(pl.multiple_of(i * wc, wc), wc)
        product = jnp.dot(xin[...], ow[:, at], preferred_element_type=F32)
        part32[i] = product
        part16[i] = product.astype(BF16)
        for d in range(1, n):
            rs_copy(i, d).start()

    for i in range(NC):
        at = slice(i * wc, (i + 1) * wc)
        total = part32[i, rows(t, R)]
        for d in range(1, n):
            rs_copy(i, d).wait_recv()
            total += rs[i, d - 1].astype(F32)
        state[:, at] = res_ref[:, at].astype(F32) + total

    def sq_copy(d):
        return remote(sqs.at[j], sqs.at[j], sq_send.at[d - 1], sq_recv.at[j], sec=sec_at(d))

    def sq_arrive(jj):
        return remote(sqs.at[jj], sqs.at[jj], sq_send.at[0], sq_recv.at[jj], sec=sec_at(1))

    squares = jnp.sum(state[...] * state[...], axis=1, keepdims=True)
    sqs[j] = jnp.broadcast_to(squares, (R, 128))
    for d in range(1, s):
        sq_copy(d).start()
    for d in range(1, s):
        sq_arrive(sec_at(d)).wait_recv()
    total = sqs[0]
    for jj in range(1, s):
        total += sqs[jj]
    scale = lax.rsqrt(total[:, :1] / (W * s) + EPSILON)
    nf[rows(t, R)] = (state[...] * scale * gain_ref[...]).astype(BF16)

    def nf_copy(d):
        return remote(
            nf.at[rows(t, R)], nf.at[rows(t, R)], nf_send.at[d - 1], nf_recv.at[t], tp=tp_at(d)
        )

    def nf_arrive(tt):
        return remote(
            nf.at[rows(tt, R)], nf.at[rows(tt, R)], nf_send.at[0], nf_recv.at[tt], tp=tp_at(1)
        )

    for d in range(1, n):
        nf_copy(d).start()
    acc[...] = jnp.zeros_like(acc)
    for d in range(1, n):
        nf_arrive(tp_at(d)).wait_recv()

    def g_copy(k):
        return remote(gsend.at[k], grecv.at[k], g_send.at[k], g_recv.at[k], sec=mate)

    def x_copy(k, d):
        return remote(
            xsend.at[k, d - 1], xrecv.at[k, d - 1], x_send.at[k, d - 1], x_recv.at[k, d - 1],
            sec=x_at(d) * 2 + c,
        )

    def h_mate(k, jj):
        at = hid.at[k, rows(jj, Q)]
        return remote(at, at, h_send.at[k, jj], h_recv.at[k, jj], sec=mate)

    def h_x(k, d):
        at = hid.at[k, rows(j, Q)]
        return remote(at, at, h_send.at[k, s - 1 + d], h_recv.at[k, j], sec=x_at(d) * 2 + c)

    @pl.loop(0, K + LAG_DOWN)
    def _(step):
        @pl.when(step < K)
        def _():
            k = step
            slot = lax.rem(k, 2)
            gw_copy(k).wait()
            uw_copy(k).wait()
            gu32[slot, :, :fc] = jnp.dot(nf[...], gw[k], preferred_element_type=F32)
            gu32[slot, :, fc:] = jnp.dot(nf[...], uw[k], preferred_element_type=F32)
            for xx in range(X):
                gsend[k, xx] = gu32[slot, rows(2 * xx + 1 - c, Q)].astype(BF16)
            g_copy(k).start()

        @pl.when((step >= LAG_SUM) & (step < K + LAG_SUM))
        def _():
            k = step - LAG_SUM
            slot = lax.rem(k, 2)
            g_copy(k).wait_recv()
            for d in range(1, X):
                xx = x_at(d)
                both = gu32[slot, rows(2 * xx + c, Q)] + grecv[k, xx].astype(F32)
                xsend[k, d - 1] = both.astype(BF16)
                x_copy(k, d).start()
            gown[lax.rem(k, OWN_RING)] = gu32[slot, rows(j, Q)] + grecv[k, x].astype(F32)

        @pl.when((step >= LAG_HIDDEN) & (step < K + LAG_HIDDEN))
        def _():
            k = step - LAG_HIDDEN
            both = gown[lax.rem(k, OWN_RING)]
            for d in range(1, X):
                x_copy(k, d).wait_recv()
                both += xrecv[k, d - 1].astype(F32)
            gate = both[:, :fc]
            hid[k, rows(j, Q)] = (gate / (1.0 + jnp.exp(-gate)) * both[:, fc:]).astype(BF16)
            for d in range(1, X):
                h_x(k, d).start()
            h_mate(k, j).start()

        @pl.when((step >= LAG_FORWARD) & (step < K + LAG_FORWARD))
        def _():
            k = step - LAG_FORWARD
            for d in range(1, X):
                jj = x_at(d) * 2 + c
                h_mate(k, jj).wait_recv()
                h_mate(k, jj).start()

        @pl.when(step >= LAG_DOWN)
        def _():
            k = step - LAG_DOWN
            dw_copy(k).wait()
            for d in range(X):
                h_mate(k, x_at(d) * 2 + (1 - c)).wait_recv()
            acc[...] += jnp.dot(hid[k], dw[k], preferred_element_type=F32)

    def d_copy(d):
        return remote(
            dsend.at[rows(tp_at(d), R)], drecv.at[d - 1], d_send.at[d - 1], d_recv.at[d - 1],
            tp=tp_at(d),
        )

    dsend[...] = acc[...].astype(BF16)
    for d in range(1, n):
        d_copy(d).start()
    final = state[...] + acc[rows(t, R)]
    for d in range(1, n):
        d_copy(d).wait_recv()
        final += drecv[d - 1].astype(F32)
    fin[...] = final.reshape(s, r, W).astype(BF16)

    def f_copy(d):
        return remote(
            fin.at[sec_at(d)], outs.at[j], f_send.at[d - 1], f_recv.at[j], sec=sec_at(d)
        )

    def f_arrive(jj):
        return remote(fin.at[jj], outs.at[jj], f_send.at[0], f_recv.at[jj], sec=sec_at(1))

    for d in range(1, s):
        f_copy(d).start()
    outs[j] = fin[j]
    for d in range(1, s):
        f_arrive(sec_at(d)).wait_recv()
    for jj in range(s):
        out_ref[:, jj * W:(jj + 1) * W] = outs[jj]

    for d in range(1, n):
        a1(d).wait_send()
        nf_copy(d).wait_send()
        d_copy(d).wait_send()
    for d in range(1, s):
        sq_copy(d).wait_send()
        f_copy(d).wait_send()
    for d in range(n):
        tt = tp_at(d)
        for e in range(1, X):
            a2_x(tt, e, d == 0).wait_send()
            a2_mate(tt, x_at(e) * 2 + c).wait_send()
        a2_mate(tt, j, d == 0).wait_send()
    for i in range(NC):
        for d in range(1, n):
            rs_copy(i, d).wait_send()

    @pl.loop(0, K)
    def _(k):
        g_copy(k).wait_send()
        for d in range(1, X):
            x_copy(k, d).wait_send()
            h_x(k, d).wait_send()
            h_mate(k, x_at(d) * 2 + c).wait_send()
        h_mate(k, j).wait_send()


def layer(n, s, attended, rest, gain, out_weight, gate_weight, up_weight, down_weight):
    r, D = attended.shape
    X = s // 2
    R = s * r
    M = n * R
    Q = n * r
    C, W = out_weight.shape
    F = gate_weight.shape[1]
    K = pieces(F)
    fc = F // K
    NC = pieces(W)
    wc = W // NC
    XP = max(X - 1, 1)
    dma = pltpu.SemaphoreType.DMA
    vmem = pl.BlockSpec(memory_space=pltpu.VMEM)
    hbm = pl.BlockSpec(memory_space=pl.ANY)
    return pl.pallas_call(
        functools.partial(layer_kernel, n, s, r),
        out_shape=jax.ShapeDtypeStruct((r, D), BF16),
        in_specs=[vmem] * 3 + [hbm] * 4,
        out_specs=vmem,
        scratch_shapes=[
            pltpu.VMEM((C, W), BF16),
            pltpu.VMEM((K, W, fc), BF16),
            pltpu.VMEM((K, W, fc), BF16),
            pltpu.VMEM((K, fc, W), BF16),
            pltpu.VMEM((n, s, r, C), BF16),
            pltpu.VMEM((M, C), BF16),
            pltpu.VMEM((NC, M, wc), F32),
            pltpu.VMEM((NC, M, wc), BF16),
            pltpu.VMEM((NC, n - 1, R, wc), BF16),
            pltpu.VMEM((R, W), F32),
            pltpu.VMEM((s, R, 128), F32),
            pltpu.VMEM((M, W), BF16),
            pltpu.VMEM((2, M, 2 * fc), F32),
            pltpu.VMEM((K, X, Q, 2 * fc), BF16),
            pltpu.VMEM((K, X, Q, 2 * fc), BF16),
            pltpu.VMEM((OWN_RING, Q, 2 * fc), F32),
            pltpu.VMEM((K, XP, Q, 2 * fc), BF16),
            pltpu.VMEM((K, XP, Q, 2 * fc), BF16),
            pltpu.VMEM((K, M, fc), BF16),
            pltpu.VMEM((M, W), F32),
            pltpu.VMEM((M, W), BF16),
            pltpu.VMEM((n - 1, R, W), BF16),
            pltpu.VMEM((s, r, W), BF16),
            pltpu.VMEM((s, r, W), BF16),
            dma((4,)), dma((K,)), dma((K,)), dma((K,)), dma,
            dma((n - 1,)), dma((n, s + XP)), dma((n, s)),
            dma((NC, n - 1)), dma((NC, n - 1)),
            dma((s - 1,)), dma((s,)),
            dma((n - 1,)), dma((n,)),
            dma((K,)), dma((K,)),
            dma((K, XP)), dma((K, XP)),
            dma((K, s + XP)), dma((K, s)),
            dma((n - 1,)), dma((n - 1,)),
            dma((s - 1,)), dma((s,)),
        ],
        compiler_params=pltpu.CompilerParams(
            collective_id=0, has_side_effects=True, vmem_limit_bytes=67043328
        ),
        name="layer",
    )(attended, rest, gain, out_weight, gate_weight, up_weight, down_weight)


def local(
    queries,
    keys,
    values,
    lengths,
    batch_of_slot,
    residual,
    out_weight,
    norm_gain,
    gate_weight,
    up_weight,
    down_weight,
):
    r = queries.shape[0]
    n = lax.axis_size("tp")
    s = lax.axis_size("sec")
    t = lax.axis_index("tp")
    attended = attend(queries, keys, values, lengths)
    slots = batch_of_slot.reshape(s, n, r)
    own_slots = lax.dynamic_index_in_dim(slots, t, 1, keepdims=False).reshape(s * r)
    rest = jnp.take(residual, own_slots, axis=0)
    return layer(
        n, s, attended, rest, norm_gain.reshape(1, -1),
        out_weight, gate_weight, up_weight, down_weight,
    )


def solution(mesh):
    return jax.shard_map(
        local,
        mesh=mesh,
        in_specs=(
            P(("parts", "sec", "tp"), None),
            P(("parts", "sec", "tp"), None, None),
            P(("parts", "sec", "tp"), None, None),
            P(("parts", "sec", "tp")),
            P("parts"),
            P("parts", "sec"),
            P("tp", "sec"),
            P("sec"),
            P("sec", "tp"),
            P("sec", "tp"),
            P("tp", "sec"),
        ),
        out_specs=P(("parts", "sec", "tp"), None),
        check_vma=False,
    )
```

time: 241 us -> 92.8 us (0.39); the launches traced: 236 us -> 92.7 us
  waiting for transfers between devices: 153 us -> 0 us
  Pallas kernels: 0 us -> 80.8 us
  blocking collectives: 28.9 us -> 0 us
  matrix products: 33.7 us -> 6.53 us
  between operations: 13.2 us -> 0.03 us
  other arithmetic: 5.07 us -> 0.75 us
    psum x2 -> x0, waiting for transfers between devices: 128 us -> none  [the longest x1 78.3 us: local(): gate_full, up_full = lax.psum((gate_part, up_part), 'sec')]
    pallas_call x0 -> x1, Pallas kernels: none -> 80.8 us  [layer(): pl.pallas_call(functools.partial(layer_kernel, n, s, r), out_shape=jax.Sh...]
    dot_general x4 -> x0, matrix products: 27.2 us -> none  [the longest x1 9.5 us: local(): jnp.dot(hidden_units, down_weight, preferred_element_type=jnp.float32)]
    reduce_scatter x1 -> x0, waiting for transfers between devices: 24.9 us -> none  [local(): lax.psum_scatter(jnp.dot(hidden_units, down_weight, preferred_element_typ...]
    all_to_all x2 -> x0, blocking collectives: 15.2 us -> none  [the longest x1 8.02 us: local(): lax.all_to_all(attended, 'tp', split_axis=1, concat_axis=0, tiled=True)]
    all_gather x1 -> x0, blocking collectives: 8.24 us -> none  [local(): lax.all_gather(columns_in, 'sec', axis=1, tiled=True)]
    psum x1 -> x0, blocking collectives: 5.49 us -> none  [normalize(): totals = lax.psum(squares, 'sec')]
    reduce_sum x1 -> x0, other arithmetic: 2.61 us -> none  [normalize(): squares = jnp.sum(hidden_state * hidden_state, axis=-1)]
  transfers between devices with their start and end apart: 3 -> 0, of which waited for: 3 -> 0; matrix products, arithmetic and copies ran while one was open for 0% -> 0% of each run, Pallas kernels for 0% -> 0%
where the time goes in v1:
time: 92.8 us; the launch traced here: 92.7 us
  Pallas kernels  80.8 us (87%)
  matrix products  6.53 us (7%)
  local copies, waits for them, and re-layouts  4.55 us (5%)
    pallas_call x1, Pallas kernels, layer(): pl.pallas_call(functools.partial(layer_kernel, n, s, r), out_shape=jax.Sh...  80.8 us
    sub x1, matrix products, attend(): weights = jnp.exp(scores - row_max)  3.55 us
    dot_general x1, matrix products, attend(): jnp.einsum('rkgp,rpkd->rkgd', probabilities, value_table, preferred_eleme...  2.98 us
    unnamed x6, local copies, waits for them, and re-layouts  2.33 us

profile of v1, /device:TPU:29, one launch (start us, length us, event | category | flops | bytes accessed | tf_op | source)
XLA Modules:
  0.0 92.7 jit_solution(6686899312759626765)
XLA Ops:
  0.0 3.5 %fusion.25 = (f32[8,8,8]{2,1,0:T(8,128)S(1)}, f32[8,8,8,256]{3,2,1,0:T(8,128)S(1)}) fusion(s32[8]{0:T(128)} %param.14, bf16[8,8,8,128]{3,0,2,1:T(8,128)(2,1)} %bitcast.39, bf16[8,256,1024]{2,1,0:T(8,128)(2,1)} %param.12), kind=kOutput, calls=%fused_computation.27 | convolution fusion | flops 34210048 | bytes 4851744 | tf_op jit(solution)/shard_map/sub | solution.py:35
  3.5 0.0 copy-start.1
  3.6 0.0 copy-start
  3.6 3.0 %fusion.18 = bf16[1,8,64,128]{3,2,1,0:T(8,128)(2,1)S(1)} fusion(f32[8,8,8,256]{3,2,1,0:T(8,128)S(1)} %get-tuple-element.8, f32[8,8,8]{2,1,0:T(8,128)S(1)} %get-tuple-element.7, bf16[8,256,1024]{2,1,0:T(8,128)(2,1)} %param.13), kind=kOutput, calls=%fused_computation.13 | convolution fusion | flops 33882112 | bytes 4851712 | tf_op jit(solution)/shard_map/rkgp,rpkd->rkgd/dot_general | solution.py:37
  6.5 0.8 copy.41
  7.3 0.0 copy-done.1
  7.3 0.1 reshape.65
  7.4 0.6 broadcast.36
  8.0 0.7 fusion.24
  8.7 0.1 reshape.67
  8.8 0.0 copy-done
  8.8 0.7 gather_fusion
  9.5 0.1 reshape.66
  9.6 0.7 broadcast_select_fusion.res_ref
  10.3 80.8 %layer.1 = bf16[8,8192]{1,0:T(8,128)(2,1)} custom-call(bf16[8,8192]{1,0:T(8,128)(2,1)} %bitcast.36, bf16[32,2048]{1,0:T(8,128)(2,1)} %broadcast_select_fusion.res_ref, f32[1,2048]{1,0:T(1,128)} %bitcast.38, bf16[2048,2048]{1,0:T(8,128)(2,1)} %ow_hbm.1, bf16[2048,3584]{1,0:T(8,128)(2,1)} %gw_hbm.1, bf16[2048,3584]{1,0:T(8,128)(2,1)} %uw_hbm.1, ...), custom_call_target="tpu_custom_call" | custom-call | tf_op jit(solution)/shard_map/layer/pallas_call | solution.py:374
  91.1 1.6 %copy.43 = bf16[8,8192]{1,0:T(8,128)(2,1)} copy(bf16[8,8192]{1,0:T(8,128)(2,1)} %layer.1) | data formatting | bytes 262144
  (3 shorter events, 0.0 us)
Async XLA Ops:
  3.5 3.7 %copy-start.1 = (s32[128]{0:T(128)S(1)}, s32[128]{0:T(128)}, u32[]{:S(2)}) copy-start(s32[128]{0:T(128)} %param.15) | copy-start | bytes 1540
  3.6 5.2 %copy-start = (bf16[128,2048]{1,0:T(8,128)(2,1)S(1)}, bf16[128,2048]{1,0:T(8,128)(2,1)}, u32[]{:S(2)}) copy-start(bf16[128,2048]{1,0:T(8,128)(2,1)} %param.16) | copy-start | bytes 1572868

commit v2 on v1

--- a/solution.py
+++ b/solution.py
@@ -18,39 +18,17 @@
 OWN_RING = 4
 
 
-def attend(queries, keys, values, lengths):
-    request_list = queries.shape[0]
-    every_position = keys.shape[1]
-    group_width = QUERY_HEADS // KEY_VALUE_HEADS
-    query_table = queries.reshape(request_list, KEY_VALUE_HEADS, group_width, HEAD_WIDTH)
-    key_table = keys.reshape(request_list, every_position, KEY_VALUE_HEADS, HEAD_WIDTH)
-    value_table = values.reshape(request_list, every_position, KEY_VALUE_HEADS, HEAD_WIDTH)
-    scores = jnp.einsum(
-        "rkgd,rpkd->rkgp", query_table, key_table, preferred_element_type=jnp.float32
-    ) * HEAD_WIDTH ** (-0.5)
-    positions = lax.broadcasted_iota(jnp.int32, scores.shape, 3)
-    in_cache = positions < lengths[:, None, None, None]
-    scores = jnp.where(in_cache, scores, -jnp.inf)
-    row_max = jnp.max(scores, axis=3, keepdims=True)
-    weights = jnp.exp(scores - row_max)
-    probabilities = (weights / jnp.sum(weights, axis=3, keepdims=True)).astype(jnp.bfloat16)
-    attended = jnp.einsum(
-        "rkgp,rpkd->rkgd", probabilities, value_table, preferred_element_type=jnp.float32
-    )
-    return attended.astype(jnp.bfloat16).reshape(request_list, QUERY_HEADS * HEAD_WIDTH)
-
-
 def pieces(size):
     return size // 512 if size % 512 == 0 else size // 128
 
 
 def layer_kernel(
     n, s, r,
-    att_ref, res_ref, gain_ref, ow_hbm, gw_hbm, uw_hbm, dw_hbm,
+    query_ref, length_ref, slot_ref, gain_ref, key_hbm, value_hbm, res_hbm, ow_hbm, gw_hbm, uw_hbm, dw_hbm,
     out_ref,
-    ow, gw, uw, dw, cols, xin, part32, part16, rs, state, sqs, nf,
-    gu32, gsend, grecv, gown, xsend, xrecv, hid, acc, dsend, drecv, fin, outs,
-    ow_sem, gw_sem, uw_sem, dw_sem, own_sem,
+    ow, gw, uw, dw, att_ref, q32, o32, cols, xin, part32, part16, rs, state, sqs, nf,
+    gu32, gsend, grecv, gown, xsend, xrecv, hid, acc, dsend, drecv, fin, outs, cache,
+    kv_sem, res_sem, ow_sem, gw_sem, uw_sem, dw_sem, own_sem,
     a1_send, a2_send, a_recv, rs_send, rs_recv, sq_send, sq_recv, nf_send, nf_recv,
     g_send, g_recv, x_send, x_recv, h_send, h_recv, d_send, d_recv, f_send, f_recv,
 ):
@@ -102,6 +80,45 @@
     def dw_copy(k):
         return pltpu.make_async_copy(dw_hbm.at[rows(k, fc)], dw.at[k], dw_sem.at[k])
 
+    P_, KW = key_hbm.shape[1:]
+    G = KEY_VALUE_HEADS // 2
+    group_width = QUERY_HEADS // KEY_VALUE_HEADS
+    heads = 2 * group_width
+    per = n // G
+    first = t * G // n
+
+    def group(i):
+        return lax.rem(first + 1 + i, G)
+
+    def columns(g):
+        return pl.ds(pl.multiple_of(g * 2 * HEAD_WIDTH, 2 * HEAD_WIDTH), 2 * HEAD_WIDTH)
+
+    def block(b, g):
+        if cache.shape[0] > 1:
+            return cache.at[b, :, columns(g)]
+        high, wide = fc // P_, W // KW
+        spot, rest = b // (high * wide), b % (high * wide)
+        offset = (rest % wide) * KW
+        at = pl.ds(pl.multiple_of(offset + g * 2 * HEAD_WIDTH, 2 * HEAD_WIDTH), 2 * HEAD_WIDTH)
+        return dw.at[spot, pl.ds((rest // wide) * P_, P_), at]
+
+    def key_copy(i, g):
+        return pltpu.make_async_copy(key_hbm.at[i, :, columns(g)], block(i, g), kv_sem.at[g, i])
+
+    def value_copy(i, g):
+        return pltpu.make_async_copy(
+            value_hbm.at[i, :, columns(g)], block(r + i, g), kv_sem.at[g, r + i]
+        )
+
+    @pl.loop(0, G)
+    def _(step):
+        g = group(step)
+        for i in range(r):
+            key_copy(i, g).start()
+            value_copy(i, g).start()
+
+    res_copy = pltpu.make_async_copy(res_hbm, dsend, res_sem)
+    res_copy.start()
     for i in range(4):
         ow_copy(i).start()
 
@@ -110,13 +127,19 @@
         pl.semaphore_signal(barrier, inc=1, device_id={"tp": tp_at(d)}, device_id_type=MESH)
     for d in range(1, s):
         pl.semaphore_signal(barrier, inc=1, device_id={"sec": sec_at(d)}, device_id_type=MESH)
+    for h in range(QUERY_HEADS):
+        at = slice(h * HEAD_WIDTH, (h + 1) * HEAD_WIDTH)
+        q32[:, h, :] = query_ref[:, at].astype(F32)
+    for k in range(K):
+        gw_copy(k).start()
+        uw_copy(k).start()
     pl.semaphore_wait(barrier, n + s - 2)
 
     def feature(tt):
         return att_ref.at[:, pl.ds(pl.multiple_of(tt * C, C), C)]
 
-    def a1(d):
-        return remote(feature(tp_at(d)), cols.at[t, j], a1_send.at[d - 1], a_recv.at[t, j], tp=tp_at(d))
+    def a1(tt):
+        return remote(feature(tt), cols.at[t, j], a1_send.at[tt], a_recv.at[t, j], tp=tt)
 
     def a1_arrive(tt):
         return remote(cols.at[tt, j], cols.at[tt, j], a1_send.at[0], a_recv.at[tt, j], tp=tp_at(1))
@@ -133,16 +156,42 @@
             a_recv.at[tt, j], sec=x_at(d) * 2 + c,
         )
 
-    for d in range(1, n):
-        a1(d).start()
+    @pl.loop(0, G)
+    def _(step):
+        g = group(step)
+        upper = lax.broadcasted_iota(jnp.int32, (heads, HEAD_WIDTH), 0) < group_width
+        positions = lax.broadcasted_iota(jnp.int32, (heads, P_), 1)
+        for i in range(r):
+            key_copy(i, g).wait()
+            value_copy(i, g).wait()
+        for i in range(r):
+            query = q32[i, rows(g, heads)]
+            query = jnp.concatenate(
+                [jnp.where(upper, query, 0.0), jnp.where(upper, 0.0, query)], axis=1
+            ).astype(BF16)
+            scores = lax.dot_general(
+                query, block(i, g)[...], (((1,), (1,)), ((), ())), preferred_element_type=F32
+            ) * HEAD_WIDTH ** (-0.5)
+            scores = jnp.where(positions < length_ref[i], scores, -jnp.inf)
+            weights = jnp.exp(scores - jnp.max(scores, axis=1, keepdims=True))
+            probs = (weights / jnp.sum(weights, axis=1, keepdims=True)).astype(BF16)
+            both = jnp.dot(probs, block(r + i, g)[...], preferred_element_type=F32)
+            o32[i] = jnp.where(upper, both[:, :HEAD_WIDTH], both[:, HEAD_WIDTH:])
+        for h in range(heads):
+            at = pl.ds(pl.multiple_of((g * heads + h) * HEAD_WIDTH, HEAD_WIDTH), HEAD_WIDTH)
+            att_ref[:, at] = o32[:, h, :].astype(BF16)
+        for e in range(per):
+            tt = g * per + e
+
+            @pl.when(tt != t)
+            def _():
+                a1(tt).start()
+
     own_copy = pltpu.make_async_copy(feature(t), cols.at[t, j], own_sem)
     own_copy.start()
     for d in range(1, X):
         a2_x(t, d, True).start()
     a2_mate(t, j, True).start()
-    for k in range(K):
-        gw_copy(k).start()
-        uw_copy(k).start()
     for k in range(K):
         dw_copy(k).start()
     for d in range(1, n):
@@ -183,13 +232,26 @@
         for d in range(1, n):
             rs_copy(i, d).start()
 
+    slot = (
+        lax.broadcasted_iota(jnp.int32, (s, r, M), 0) * (n * r) + t * r
+        + lax.broadcasted_iota(jnp.int32, (s, r, M), 1)
+    )
+    mine = jnp.where(lax.broadcasted_iota(jnp.int32, (s, r, M), 2) == slot, 1.0, 0.0)
+    batch = lax.broadcasted_iota(jnp.int32, (M, M), 0)
+    held = jnp.where(batch == slot_ref[...], 1.0, 0.0).astype(BF16)
+    pick = lax.dot_general(
+        mine.reshape(R, M).astype(BF16), held, (((1,), (1,)), ((), ())),
+        preferred_element_type=F32,
+    ).astype(BF16)
+    res_copy.wait()
+    state[...] = jnp.dot(pick, dsend[...], preferred_element_type=F32)
     for i in range(NC):
         at = slice(i * wc, (i + 1) * wc)
         total = part32[i, rows(t, R)]
         for d in range(1, n):
             rs_copy(i, d).wait_recv()
             total += rs[i, d - 1].astype(F32)
-        state[:, at] = res_ref[:, at].astype(F32) + total
+        state[:, at] = state[:, at] + total
 
     def sq_copy(d):
         return remote(sqs.at[j], sqs.at[j], sq_send.at[d - 1], sq_recv.at[j], sec=sec_at(d))
@@ -329,7 +391,7 @@
         out_ref[:, jj * W:(jj + 1) * W] = outs[jj]
 
     for d in range(1, n):
-        a1(d).wait_send()
+        a1(tp_at(d)).wait_send()
         nf_copy(d).wait_send()
         d_copy(d).wait_send()
     for d in range(1, s):
@@ -355,8 +417,10 @@
         h_mate(k, j).wait_send()
 
 
-def layer(n, s, attended, rest, gain, out_weight, gate_weight, up_weight, down_weight):
-    r, D = attended.shape
+def layer(n, s, queries, lengths, slots, gain, keys, values, residual, out_weight, gate_weight, up_weight, down_weight):
+    r, D = queries.shape
+    P_, KW = keys.shape[1:]
+    assert n % (KEY_VALUE_HEADS // 2) == 0
     X = s // 2
     R = s * r
     M = n * R
@@ -368,19 +432,24 @@
     NC = pieces(W)
     wc = W // NC
     XP = max(X - 1, 1)
+    inside = fc % P_ == 0 and W % KW == 0 and K * (fc // P_) * (W // KW) >= 2 * r
+    cache = (1, 16, 128) if inside else (2 * r, P_, KW)
     dma = pltpu.SemaphoreType.DMA
     vmem = pl.BlockSpec(memory_space=pltpu.VMEM)
     hbm = pl.BlockSpec(memory_space=pl.ANY)
     return pl.pallas_call(
         functools.partial(layer_kernel, n, s, r),
         out_shape=jax.ShapeDtypeStruct((r, D), BF16),
-        in_specs=[vmem] * 3 + [hbm] * 4,
+        in_specs=[vmem, pl.BlockSpec(memory_space=pltpu.SMEM), vmem, vmem] + [hbm] * 7,
         out_specs=vmem,
         scratch_shapes=[
             pltpu.VMEM((C, W), BF16),
             pltpu.VMEM((K, W, fc), BF16),
             pltpu.VMEM((K, W, fc), BF16),
             pltpu.VMEM((K, fc, W), BF16),
+            pltpu.VMEM((r, D), BF16),
+            pltpu.VMEM((r, QUERY_HEADS, HEAD_WIDTH), F32),
+            pltpu.VMEM((r, 2 * QUERY_HEADS // KEY_VALUE_HEADS, HEAD_WIDTH), F32),
             pltpu.VMEM((n, s, r, C), BF16),
             pltpu.VMEM((M, C), BF16),
             pltpu.VMEM((NC, M, wc), F32),
@@ -401,8 +470,10 @@
             pltpu.VMEM((n - 1, R, W), BF16),
             pltpu.VMEM((s, r, W), BF16),
             pltpu.VMEM((s, r, W), BF16),
+            pltpu.VMEM(cache, BF16),
+            dma((KEY_VALUE_HEADS // 2, 2 * r)), dma,
             dma((4,)), dma((K,)), dma((K,)), dma((K,)), dma,
-            dma((n - 1,)), dma((n, s + XP)), dma((n, s)),
+            dma((n,)), dma((n, s + XP)), dma((n, s)),
             dma((NC, n - 1)), dma((NC, n - 1)),
             dma((s - 1,)), dma((s,)),
             dma((n - 1,)), dma((n,)),
@@ -416,7 +487,7 @@
             collective_id=0, has_side_effects=True, vmem_limit_bytes=67043328
         ),
         name="layer",
-    )(attended, rest, gain, out_weight, gate_weight, up_weight, down_weight)
+    )(queries, lengths, slots, gain, keys, values, residual, out_weight, gate_weight, up_weight, down_weight)
 
 
 def local(
@@ -432,16 +503,9 @@
     up_weight,
     down_weight,
 ):
-    r = queries.shape[0]
-    n = lax.axis_size("tp")
-    s = lax.axis_size("sec")
-    t = lax.axis_index("tp")
-    attended = attend(queries, keys, values, lengths)
-    slots = batch_of_slot.reshape(s, n, r)
-    own_slots = lax.dynamic_index_in_dim(slots, t, 1, keepdims=False).reshape(s * r)
-    rest = jnp.take(residual, own_slots, axis=0)
     return layer(
-        n, s, attended, rest, norm_gain.reshape(1, -1),
+        lax.axis_size("tp"), lax.axis_size("sec"), queries, lengths,
+        batch_of_slot.reshape(1, -1), norm_gain.reshape(1, -1), keys, values, residual,
         out_weight, gate_weight, up_weight, down_weight,
     )
 

time: 92.8 us -> 92.2 us (level)
  Pallas kernels: 80.8 us -> 90.4 us
  matrix products: 6.53 us -> 0 us
  local copies, waits for them, and re-layouts: 4.55 us -> 1.57 us
    pallas_call x1, Pallas kernels: 80.8 us -> 90.4 us  [layer(): pl.pallas_call(functools.partial(layer_kernel, n, s, r), out_shape=jax.Sh...]
    sub x1 -> x0, matrix products: 3.55 us -> none  [attend(): weights = jnp.exp(scores - row_max)]
    dot_general x1 -> x0, matrix products: 2.98 us -> none  [attend(): jnp.einsum('rkgp,rpkd->rkgd', probabilities, value_table, preferred_eleme...]
    dynamic_slice x2 -> x0, local copies, waits for them, and re-layouts: 1.31 us -> none  [local(): lax.dynamic_index_in_dim(slots, t, 1, keepdims=False).reshape(s * r)]
    unnamed x6 -> x1, local copies, waits for them, and re-layouts: 2.33 us -> 1.57 us
where the time goes in v2:
time: 92.2 us; the launch traced here: 92 us
  Pallas kernels  90.4 us (98%)
  local copies, waits for them, and re-layouts  1.57 us (2%)
    pallas_call x1, Pallas kernels, layer(): pl.pallas_call(functools.partial(layer_kernel, n, s, r), out_shape=jax.Sh...  90.4 us

profile of v2, /device:TPU:29, one launch (start us, length us, event | category | flops | bytes accessed | tf_op | source)
XLA Modules:
  0.0 92.0 jit_solution(4739886125144598038)
XLA Ops:
  0.0 90.4 %layer.1 = bf16[8,8192]{1,0:T(8,128)(2,1)} custom-call(bf16[8,8192]{1,0:T(8,128)(2,1)} %query_ref.1, s32[8]{0:T(128)} %length_ref.1, s32[1,128]{1,0:T(1,128)} %bitcast.3, f32[1,2048]{1,0:T(1,128)} %bitcast.2, bf16[8,256,1024]{2,1,0:T(8,128)(2,1)} %key_hbm.1, bf16[8,256,1024]{2,1,0:T(8,128)(2,1)} %value_hbm.1, bf16[128,2048]{1,0:T(8,128)(2,1)} %res_hbm.1, ...), custom_call_target="tpu_custom_call" | custom-call | tf_op jit(solution)/shard_map/layer/pallas_call | solution.py:440
  90.4 1.6 %copy.13 = bf16[8,8192]{1,0:T(8,128)(2,1)} copy(bf16[8,8192]{1,0:T(8,128)(2,1)} %layer.1) | data formatting | bytes 262144

commit v3 on v2

--- a/solution.py
+++ b/solution.py
@@ -164,18 +164,23 @@
         for i in range(r):
             key_copy(i, g).wait()
             value_copy(i, g).wait()
+        scores = []
         for i in range(r):
             query = q32[i, rows(g, heads)]
             query = jnp.concatenate(
                 [jnp.where(upper, query, 0.0), jnp.where(upper, 0.0, query)], axis=1
             ).astype(BF16)
-            scores = lax.dot_general(
+            one = lax.dot_general(
                 query, block(i, g)[...], (((1,), (1,)), ((), ())), preferred_element_type=F32
             ) * HEAD_WIDTH ** (-0.5)
-            scores = jnp.where(positions < length_ref[i], scores, -jnp.inf)
-            weights = jnp.exp(scores - jnp.max(scores, axis=1, keepdims=True))
-            probs = (weights / jnp.sum(weights, axis=1, keepdims=True)).astype(BF16)
-            both = jnp.dot(probs, block(r + i, g)[...], preferred_element_type=F32)
+            scores.append(jnp.where(positions < length_ref[i], one, -jnp.inf))
+        scores = jnp.concatenate(scores, axis=0)
+        weights = jnp.exp(scores - jnp.max(scores, axis=1, keepdims=True))
+        probs = (weights / jnp.sum(weights, axis=1, keepdims=True)).astype(BF16)
+        for i in range(r):
+            both = jnp.dot(
+                probs[i * heads:(i + 1) * heads], block(r + i, g)[...], preferred_element_type=F32
+            )
             o32[i] = jnp.where(upper, both[:, :HEAD_WIDTH], both[:, HEAD_WIDTH:])
         for h in range(heads):
             at = pl.ds(pl.multiple_of((g * heads + h) * HEAD_WIDTH, HEAD_WIDTH), HEAD_WIDTH)

time: 92.2 us -> 84.9 us (0.921)
  Pallas kernels: 90.4 us -> 83.2 us
    pallas_call x1, Pallas kernels: 90.4 us -> 83.2 us  [layer(): pl.pallas_call(functools.partial(layer_kernel, n, s, r), out_shape=jax.Sh...]
where the time goes in v3:
time: 84.9 us; the launch traced here: 84.8 us
  Pallas kernels  83.2 us (98%)
  local copies, waits for them, and re-layouts  1.57 us (2%)
    pallas_call x1, Pallas kernels, layer(): pl.pallas_call(functools.partial(layer_kernel, n, s, r), out_shape=jax.Sh...  83.2 us

profile of v3, /device:TPU:29, one launch (start us, length us, event | category | flops | bytes accessed | tf_op | source)
XLA Modules:
  0.0 84.8 jit_solution(4062474770898422987)
XLA Ops:
  0.0 83.2 %layer.1 = bf16[8,8192]{1,0:T(8,128)(2,1)} custom-call(bf16[8,8192]{1,0:T(8,128)(2,1)} %query_ref.1, s32[8]{0:T(128)} %length_ref.1, s32[1,128]{1,0:T(1,128)} %bitcast.3, f32[1,2048]{1,0:T(1,128)} %bitcast.2, bf16[8,256,1024]{2,1,0:T(8,128)(2,1)} %key_hbm.1, bf16[8,256,1024]{2,1,0:T(8,128)(2,1)} %value_hbm.1, bf16[128,2048]{1,0:T(8,128)(2,1)} %res_hbm.1, ...), custom_call_target="tpu_custom_call" | custom-call | tf_op jit(solution)/shard_map/layer/pallas_call | solution.py:445
  83.2 1.6 %copy.13 = bf16[8,8192]{1,0:T(8,128)(2,1)} copy(bf16[8,8192]{1,0:T(8,128)(2,1)} %layer.1) | data formatting | bytes 262144
